TPU v7x, 32 devices: a whole 2x2x4 slice. The times are simulated.
32 devices in a mesh: groups: 2 (over x), row: 16 (over z, y, core).
Axes of the slice: x: 2, y: 2, z: 4, core: 2. Of those that a mesh axis runs over, the one named last changes fastest.
Arguments:
- factor_panel: bfloat16 [32768, 2048], P(('groups', 'row')), parts along dimension 0, may hold values from -0.25 to 0.25
- pivots: float32 [4096], P('groups'), parts along dimension 0, may hold values from 1 to 1.25
- right_sides: float32 [32768, 256], P(('groups', 'row')), parts along dimension 0, may hold values from -6 to 6
- block_home: int32 [32], replicated, may hold values from 0 to 31, each once
Outputs:
- remainder: float32 [32768, 256], P('groups', 'row'), parts along dimension 0
- psf_variance: float32 [512], P(('groups', 'row')), parts along dimension 0
There are 2 independent parts, one for each index of `groups`. A program takes and returns all parts, laid end to end along the dimension named above; an argument that names none is the same for every part. Nothing has to cross between parts.
Inputs may be any that keep to these rules, and one draw needn't show every extreme that they name: block_home[g] is the stored position of global block g; position p is slot p % 2 of row device p // 2; every position holds exactly one block.
All inputs are finite; a program needn't handle non-finite values.
Results may differ from a plain program's by a relative error of at most 0.0042.
Values may be sent and summed in bfloat16 or wider, within the bound.
No kernel may reach another device: no remote copies, remote signals or barrier semaphores. Data moves between devices by JAX's collectives and lax.ppermute only.
A program may use at most 128 MiB of HBM per device.

v0:
```python
import jax
import jax.numpy as jnp
from jax import lax
from jax.sharding import PartitionSpec as P

BLOCK = 512
STEPS = 4
PANEL = 2048


def spread(value, axis, source):
    kept = jnp.where(lax.axis_index(axis) == source, value, 0).astype(value.dtype)
    return lax.psum(kept, axis)


def on_device(factor_panel, pivots, right_sides, block_home):
    slot_count = factor_panel.shape[0] // BLOCK
    columns_all = right_sides.shape[1]
    row_count = lax.axis_size("row")
    row_index = lax.axis_index("row")
    block_total = block_home.shape[0]
    positions = row_index * slot_count + jnp.arange(slot_count, dtype=jnp.int32)
    global_ids = jnp.sum(
        jnp.where(
            block_home[None, :] == positions[:, None],
            jnp.arange(block_total, dtype=jnp.int32)[None, :],
            0,
        ),
        axis=1,
    )
    partial_value = right_sides.reshape(slot_count, BLOCK, columns_all)
    factor_blocks = factor_panel.reshape(slot_count, BLOCK, PANEL)
    my_columns = columns_all // row_count
    solutions = []
    for k in range(STEPS):
        slot = block_home[k] % slot_count
        rows = lax.dynamic_index_in_dim(partial_value, slot, 0, keepdims=False)
        diag_slot = block_home[k] % slot_count
        held = lax.dynamic_index_in_dim(factor_blocks, diag_slot, 0, keepdims=False)
        diag_rows = held[:, k * BLOCK : (k + 1) * BLOCK].astype(jnp.float32)
        diag_block = jnp.tril(diag_rows, -1) + jnp.diag(pivots[k * BLOCK : (k + 1) * BLOCK])
        solution = jax.scipy.linalg.solve_triangular(diag_block, rows, lower=True).astype(
            jnp.bfloat16
        )
        solution = spread(solution, "row", block_home[k] // slot_count)
        active = (global_ids > k).astype(jnp.float32)
        product = jnp.einsum(
            "sij,jc->sic",
            factor_blocks[:, :, k * BLOCK : (k + 1) * BLOCK],
            solution,
            preferred_element_type=jnp.float32,
        )
        partial_value = partial_value - active[:, None, None] * product
        partial_value = jnp.where(
            (global_ids == k)[:, None, None], solution.astype(jnp.float32)[None], partial_value
        )
        solutions.append(solution)
    stored = lax.all_to_all(
        partial_value.reshape(slot_count * BLOCK, columns_all),
        "row",
        split_axis=1,
        concat_axis=0,
        tiled=True,
    )
    ordered = jnp.take(stored.reshape(block_total, BLOCK, my_columns), block_home, axis=0)
    remainder = ordered.reshape(block_total * BLOCK, my_columns)
    solved = remainder[: STEPS * BLOCK]
    psf_variance = jnp.mean(solved * solved, axis=0)
    return (remainder, psf_variance)


def solution(mesh):
    in_specs = (P(("groups", "row"), None), P("groups"), P(("groups", "row"), None), P())
    out_specs = (P("groups", "row"), P(("groups", "row")))
    return jax.shard_map(
        on_device, mesh=mesh, in_specs=in_specs, out_specs=out_specs, check_vma=False
    )
```

profile of v0, /device:TPU:9, one launch (start us, length us, event | category | flops | bytes accessed | tf_op | source)
XLA Modules:
  0.0 519.9 jit_solution(8942205453289188810)
XLA Ops:
  17.5 4.6 dynamic-slice_bitcast_fusion.3
  22.1 2.0 fusion.19
  24.1 12.0 %while.8 = (s32[]{:T(128)}, f32[512,512]{1,0:T(8,128)}, s32[4,2]{0,1:T(2,128)S(1)}, f32[4,128,128]{2,1,0:T(8,128)S(1)}, s32[]{:T(128)}) while((s32[]{:T(128)}, f32[512,512]{1,0:T(8,128)}, s32[4,2]{0,1:T(2,128)S(1)}, f32[4,128,128]{2,1,0:T(8,128)S(1)}, s32[]{:T(128)}) %tuple.86), condition=%wide.while_cond, body=%wide.while_body.sunk | while | flops 2 | bytes 131181 | solution.py:42
  24.8 2.3 bitcast_dynamic-update-slice_fusion.8
  27.8 2.3 bitcast_dynamic-update-slice_fusion.8
  30.8 2.3 bitcast_dynamic-update-slice_fusion.8
  33.8 2.2 bitcast_dynamic-update-slice_fusion.8
  36.8 40.1 %custom-call.6 = f32[4,128,128]{1,2,0:T(8,128)S(1)} custom-call(f32[4,128,128]{2,1,0:T(8,128)} %copy-done.2), custom_call_target="InvertDiagBlocksLowerTriangular" | custom-call | tf_op jit(solution)/shard_map/jit(_solve_triangular)/triangular_solve | solution.py:42
  85.1 7.6 %while.9 = (s32[]{:T(128)}, f32[512,512]{1,0:T(8,128)S(1)}, s32[4,2]{0,1:T(2,128)S(1)}, f32[4,128,128]{2,1,0:T(8,128)S(1)}, s32[]{:T(128)}) while((s32[]{:T(128)}, f32[512,512]{1,0:T(8,128)S(1)}, s32[4,2]{0,1:T(2,128)S(1)}, f32[4,128,128]{2,1,0:T(8,128)S(1)}, s32[]{:T(128)}) %tuple.106), condition=%wide.while_cond.clone, body=%wide.while_body.clone.sunk | while | flops 2 | bytes 131181 | solution.py:42
  93.4 40.2 %custom-call.7 = f32[4,128,128]{1,2,0:T(8,128)S(1)} custom-call(f32[4,128,128]{2,1,0:T(8,128)} %copy-done.3), custom_call_target="InvertDiagBlocksLowerTriangular" | custom-call | tf_op jit(solution)/shard_map/jit(_solve_triangular)/triangular_solve | solution.py:42
  133.7 40.1 %all-reduce.5.cloned.1.call-done = bf16[512,256]{1,0:T(8,128)(2,1)} async-done(((bf16[512,256]{1,0:T(8,128)(2,1)}), bf16[512,256]{1,0:T(8,128)(2,1)}) %all-reduce.5.cloned.1.call-update) | async-done | bytes 262160 | tf_op jit(solution)/shard_map/psum | solution.py:13
  183.8 11.1 %while.10 = (s32[]{:T(128)}, f32[512,512]{1,0:T(8,128)}, s32[4,2]{0,1:T(2,128)S(1)}, f32[4,128,128]{2,1,0:T(8,128)S(1)}, s32[]{:T(128)}) while((s32[]{:T(128)}, f32[512,512]{1,0:T(8,128)}, s32[4,2]{0,1:T(2,128)S(1)}, f32[4,128,128]{2,1,0:T(8,128)S(1)}, s32[]{:T(128)}) %tuple.107), condition=%wide.while_cond.clone.1, body=%wide.while_body.clone.1.sunk | while | flops 2 | bytes 131181 | solution.py:42
  184.4 2.2 bitcast_dynamic-update-slice_fusion.10
  187.2 2.2 bitcast_dynamic-update-slice_fusion.10
  190.0 2.2 bitcast_dynamic-update-slice_fusion.10
  192.8 2.1 bitcast_dynamic-update-slice_fusion.10
  195.5 39.3 %custom-call.8 = f32[4,128,128]{1,2,0:T(8,128)S(1)} custom-call(f32[4,128,128]{2,1,0:T(8,128)S(1)} %get-tuple-element.31), custom_call_target="InvertDiagBlocksLowerTriangular" | custom-call | tf_op jit(solution)/shard_map/jit(_solve_triangular)/triangular_solve | solution.py:42
  234.9 39.7 %all-reduce.7.cloned.1.call-done = bf16[512,256]{1,0:T(8,128)(2,1)} async-done(((bf16[512,256]{1,0:T(8,128)(2,1)}), bf16[512,256]{1,0:T(8,128)(2,1)}) %all-reduce.7.cloned.1.call-update) | async-done | bytes 262160 | tf_op jit(solution)/shard_map/psum | solution.py:13
  284.4 8.3 %while.11 = (s32[]{:T(128)}, f32[512,512]{1,0:T(8,128)S(1)}, s32[4,2]{0,1:T(2,128)S(1)}, f32[4,128,128]{2,1,0:T(8,128)S(1)}, s32[]{:T(128)}) while((s32[]{:T(128)}, f32[512,512]{1,0:T(8,128)S(1)}, s32[4,2]{0,1:T(2,128)S(1)}, f32[4,128,128]{2,1,0:T(8,128)S(1)}, s32[]{:T(128)}) %tuple.108), condition=%wide.while_cond.clone.2, body=%wide.while_body.clone.2.sunk | while | flops 2 | bytes 131181 | solution.py:42
  293.4 39.3 %custom-call.9 = f32[4,128,128]{1,2,0:T(8,128)S(1)} custom-call(f32[4,128,128]{2,1,0:T(8,128)S(1)} %get-tuple-element.32), custom_call_target="InvertDiagBlocksLowerTriangular" | custom-call | tf_op jit(solution)/shard_map/jit(_solve_triangular)/triangular_solve | solution.py:42
  332.7 42.4 %all-reduce.9.cloned.1.call-done = bf16[512,256]{1,0:T(8,128)(2,1)} async-done(((bf16[512,256]{1,0:T(8,128)(2,1)}), bf16[512,256]{1,0:T(8,128)(2,1)}) %all-reduce.9.cloned.1.call-update) | async-done | bytes 262160 | tf_op jit(solution)/shard_map/psum | solution.py:13
  382.2 90.3 %all-reduce.11.cloned.1.call-done = bf16[512,256]{1,0:T(8,128)(2,1)} async-done(((bf16[512,256]{1,0:T(8,128)(2,1)}), bf16[512,256]{1,0:T(8,128)(2,1)}) %all-reduce.11.cloned.1.call-update) | async-done | bytes 262160 | tf_op jit(solution)/shard_map/psum | solution.py:13
  478.1 6.5 %all-to-all-start = ((f32[1024,16,16]{0,2,1:T(8,128)}), f32[1024,16,16]{0,2,1:T(8,128)S(1)}, u32[]{:S(2)}, u32[]{:S(2)}) async-start(f32[1024,16,16]{0,2,1:T(8,128)} %all_to_all.12), calls=%async_computation | async-start | bytes 2097152 | tf_op jit(solution)/shard_map/all_to_all | solution.py:58
  484.7 24.8 %all-to-all-done = f32[1024,16,16]{0,2,1:T(8,128)S(1)} async-done(((f32[1024,16,16]{0,2,1:T(8,128)}), f32[1024,16,16]{0,2,1:T(8,128)S(1)}, u32[]{:S(2)}, u32[]{:S(2)}) %all-to-all-start) | async-done | bytes 1048608 | tf_op jit(solution)/shard_map/all_to_all | solution.py:58
  (133 shorter events, 68.3 us)
Async XLA Ops:
  7.2 166.6 %all-reduce.5.cloned.1.call-start = ((), (), s32[]{:S(2)}) async-start(), calls=%async_computation.1 | async-start | bytes 524288 | tf_op jit(solution)/shard_map/psum | solution.py:13
  22.1 54.9 %copy-start.1 = (f32[1024,256]{1,0:T(8,128)S(1)}, f32[1024,256]{1,0:T(8,128)}, u32[]{:S(2)}) copy-start(f32[1024,256]{1,0:T(8,128)} %param.8) | copy-start | bytes 3145732
  24.1 60.8 %copy-start.4 = (s32[32]{0:T(128)S(1)}, s32[32]{0:T(128)}, u32[]{:S(2)}) copy-start(s32[32]{0:T(128)} %param.9) | copy-start | bytes 388
  36.1 0.7 copy-start.2
  82.7 191.8 %all-reduce.7.cloned.1.call-start = ((), (), s32[]{:S(2)}) async-start(), calls=%async_computation.2 | async-start | bytes 524288 | tf_op jit(solution)/shard_map/psum | solution.py:13
  92.7 0.7 copy-start.3
  93.4 82.2 %copy-start = (f32[512,512]{1,0:T(8,128)}, f32[512,512]{1,0:T(8,128)S(1)}, u32[]{:S(2)}) copy-start(f32[512,512]{1,0:T(8,128)S(1)} %get-tuple-element.280) | copy-start | bytes 3145732
  183.5 191.6 %all-reduce.9.cloned.1.call-start = ((), (), s32[]{:S(2)}) async-start(), calls=%async_computation.3 | async-start | bytes 524288 | tf_op jit(solution)/shard_map/psum | solution.py:13
  284.3 188.2 %all-reduce.11.cloned.1.call-start = ((), (), s32[]{:S(2)}) async-start(), calls=%async_computation.4 | async-start | bytes 524288 | tf_op jit(solution)/shard_map/psum | solution.py:13
  478.1 31.4 %all-to-all-start = ((f32[1024,16,16]{0,2,1:T(8,128)}), f32[1024,16,16]{0,2,1:T(8,128)S(1)}, u32[]{:S(2)}, u32[]{:S(2)}) async-start(f32[1024,16,16]{0,2,1:T(8,128)} %all_to_all.12), calls=%async_computation | async-start | bytes 2097152 | tf_op jit(solution)/shard_map/all_to_all | solution.py:58
Sparse Core Ops, SparseCore 0:
  82.8 90.8 all-reduce.4
  183.6 90.8 all-reduce.6
  284.4 90.6 all-reduce.8
  382.3 90.1 all-reduce.10
where the time goes:
time: 521 us; the launch traced here: 520 us
  waiting for transfers between devices  237 us (45%)
  other arithmetic  166 us (32%)
  local copies, waits for them, and re-layouts  60.9 us (12%)
  between operations  24.4 us (5%)
  matrix products  24.3 us (5%)
  starting transfers between devices  6.81 us (1%)
    psum x4, waiting for transfers between devices, spread(): return lax.psum(kept, axis)  212 us
    another operation x6, other arithmetic, on_device(): jax.scipy.linalg.solve_triangular(diag_block, rows, lower=True)  161 us
    another operation x53, local copies, waits for them, and re-layouts, on_device(): jax.scipy.linalg.solve_triangular(diag_block, rows, lower=True)  38.8 us
    all_to_all x1, waiting for transfers between devices, on_device(): lax.all_to_all(partial_value.reshape(slot_count * BLOCK, columns_all), 'r...  24.8 us
    another operation x28, matrix products, on_device(): jax.scipy.linalg.solve_triangular(diag_block, rows, lower=True)  16.7 us
  transfers between devices with their start and end apart: 5, of which 5 were waited for; matrix products, arithmetic and copies ran while one was open for 28% of the time, Pallas kernels for 0%

commit v1 on v0

--- a/solution.py
+++ b/solution.py
@@ -10,7 +10,7 @@
 
 def spread(value, axis, source):
     kept = jnp.where(lax.axis_index(axis) == source, value, 0).astype(value.dtype)
-    return lax.psum(kept, axis)
+    return jnp.sum(lax.all_gather(kept, axis), axis=0)
 
 
 def on_device(factor_panel, pivots, right_sides, block_home):

time: 521 us -> 379 us (0.73)
  waiting for transfers between devices: 237 us -> 77.5 us
  other arithmetic: 166 us -> 178 us
  matrix products: 24.3 us -> 31.4 us
    psum x4 -> x0, waiting for transfers between devices: 212 us -> none  [spread(): return lax.psum(kept, axis)]
    all_gather x0 -> x4, waiting for transfers between devices: none -> 52.7 us  [spread(): return jnp.sum(lax.all_gather(kept, axis), axis=0)]
    reduce_sum x0 -> x4, other arithmetic: none -> 11.4 us  [spread(): return jnp.sum(lax.all_gather(kept, axis), axis=0)]
    another operation x28, matrix products: 16.7 us -> 24.1 us  [on_device(): jax.scipy.linalg.solve_triangular(diag_block, rows, lower=True)]
  transfers between devices with their start and end apart: 5 -> 5, of which waited for: 5 -> 3; matrix products, arithmetic and copies ran while one was open for 28% -> 41% of each run, Pallas kernels for 0% -> 0%
where the time goes in v1:
time: 379 us; the launch traced here: 377 us
  other arithmetic  178 us (47%)
  waiting for transfers between devices  77.5 us (20%)
  local copies, waits for them, and re-layouts  61 us (16%)
  matrix products  31.4 us (8%)
  between operations  24.6 us (6%)
  starting transfers between devices  4.17 us (1%)
    another operation x6, other arithmetic, on_device(): jax.scipy.linalg.solve_triangular(diag_block, rows, lower=True)  161 us
    all_gather x4, waiting for transfers between devices, spread(): return jnp.sum(lax.all_gather(kept, axis), axis=0)  52.7 us
    another operation x53, local copies, waits for them, and re-layouts, on_device(): jax.scipy.linalg.solve_triangular(diag_block, rows, lower=True)  39.5 us
    all_to_all x1, waiting for transfers between devices, on_device(): lax.all_to_all(partial_value.reshape(slot_count * BLOCK, columns_all), 'r...  24.8 us
    another operation x28, matrix products, on_device(): jax.scipy.linalg.solve_triangular(diag_block, rows, lower=True)  24.1 us
    reduce_sum x4, other arithmetic, spread(): return jnp.sum(lax.all_gather(kept, axis), axis=0)  11.4 us
  transfers between devices with their start and end apart: 5, of which 3 were waited for; matrix products, arithmetic and copies ran while one was open for 41% of the time, Pallas kernels for 0%

profile of v1, /device:TPU:9, one launch (start us, length us, event | category | flops | bytes accessed | tf_op | source)
XLA Modules:
  0.0 376.6 jit_solution(4993105133777063047)
XLA Ops:
  17.9 4.5 %dynamic-slice_bitcast_fusion.3 = (bf16[512,2048]{1,0:T(8,128)(2,1)S(1)}, bf16[512,2048]{1,0:T(8,128)(2,1)S(1)}, bf16[512,2048]{1,0:T(8,128)(2,1)S(1)}, bf16[512,2048]{1,0:T(8,128)(2,1)S(1)}) fusion(bf16[2,512,2048]{2,1,0:T(8,128)(2,1)} %bitcast.175, s32[]{:T(128)S(6)} %select_n.145, s32[]{:T(128)S(6)} %select_n.163, s32[]{:T(128)S(6)} %select_n.157, ...), kind=kLoop, calls=%fused_computation.12 | loop fusion | bytes 16777232 | tf_op jit(solution)/shard_map/jit(dynamic_index_in_dim)/squeeze | solution.py:39
  24.4 7.8 %while.8 = (s32[]{:T(128)}, f32[512,512]{1,0:T(8,128)S(1)}, s32[4,2]{0,1:T(2,128)S(1)}, f32[4,128,128]{2,1,0:T(8,128)S(1)}, s32[]{:T(128)}) while((s32[]{:T(128)}, f32[512,512]{1,0:T(8,128)S(1)}, s32[4,2]{0,1:T(2,128)S(1)}, f32[4,128,128]{2,1,0:T(8,128)S(1)}, s32[]{:T(128)}) %tuple.86), condition=%wide.while_cond, body=%wide.while_body.sunk | while | flops 2 | bytes 131181 | solution.py:42
  32.2 39.3 %custom-call.6 = f32[4,128,128]{1,2,0:T(8,128)S(1)} custom-call(f32[4,128,128]{2,1,0:T(8,128)S(1)} %get-tuple-element.29), custom_call_target="InvertDiagBlocksLowerTriangular" | custom-call | tf_op jit(solution)/shard_map/jit(_solve_triangular)/triangular_solve | solution.py:42
  77.9 11.7 %while.9 = (s32[]{:T(128)}, f32[512,512]{1,0:T(8,128)}, s32[4,2]{0,1:T(2,128)S(1)}, f32[4,128,128]{2,1,0:T(8,128)S(1)}, s32[]{:T(128)}) while((s32[]{:T(128)}, f32[512,512]{1,0:T(8,128)}, s32[4,2]{0,1:T(2,128)S(1)}, f32[4,128,128]{2,1,0:T(8,128)S(1)}, s32[]{:T(128)}) %tuple.106), condition=%wide.while_cond.clone, body=%wide.while_body.clone.sunk | while | flops 2 | bytes 131181 | solution.py:42
  78.6 2.3 bitcast_dynamic-update-slice_fusion.9
  81.5 2.3 bitcast_dynamic-update-slice_fusion.9
  84.4 2.3 bitcast_dynamic-update-slice_fusion.9
  89.6 40.0 %custom-call.7 = f32[4,128,128]{1,2,0:T(8,128)} custom-call(f32[4,128,128]{2,1,0:T(8,128)S(1)} %get-tuple-element.30), custom_call_target="InvertDiagBlocksLowerTriangular" | custom-call | tf_op jit(solution)/shard_map/jit(_solve_triangular)/triangular_solve | solution.py:42
  129.8 2.9 reduce_sum.67
  147.5 11.9 %while.10 = (s32[]{:T(128)}, f32[512,512]{1,0:T(8,128)}, s32[4,2]{0,1:T(2,128)S(1)}, f32[4,128,128]{2,1,0:T(8,128)S(1)}, s32[]{:T(128)}) while((s32[]{:T(128)}, f32[512,512]{1,0:T(8,128)}, s32[4,2]{0,1:T(2,128)S(1)}, f32[4,128,128]{2,1,0:T(8,128)S(1)}, s32[]{:T(128)}) %tuple.107), condition=%wide.while_cond.clone.1, body=%wide.while_body.clone.1.sunk | while | flops 2 | bytes 131181 | solution.py:42
  148.1 2.3 bitcast_dynamic-update-slice_fusion.10
  151.1 2.3 bitcast_dynamic-update-slice_fusion.10
  154.1 2.3 bitcast_dynamic-update-slice_fusion.10
  157.1 2.2 bitcast_dynamic-update-slice_fusion.10
  159.3 39.9 %custom-call.8 = f32[4,128,128]{1,2,0:T(8,128)} custom-call(f32[4,128,128]{2,1,0:T(8,128)S(1)} %get-tuple-element.31), custom_call_target="InvertDiagBlocksLowerTriangular" | custom-call | tf_op jit(solution)/shard_map/jit(_solve_triangular)/triangular_solve | solution.py:42
  199.3 2.9 reduce_sum.68
  214.9 8.4 %while.11 = (s32[]{:T(128)}, f32[512,512]{1,0:T(8,128)S(1)}, s32[4,2]{0,1:T(2,128)S(1)}, f32[4,128,128]{2,1,0:T(8,128)S(1)}, s32[]{:T(128)}) while((s32[]{:T(128)}, f32[512,512]{1,0:T(8,128)S(1)}, s32[4,2]{0,1:T(2,128)S(1)}, f32[4,128,128]{2,1,0:T(8,128)S(1)}, s32[]{:T(128)}) %tuple.108), condition=%wide.while_cond.clone.2, body=%wide.while_body.clone.2.sunk | while | flops 2 | bytes 131181 | solution.py:42
  223.3 39.9 %custom-call.9 = f32[4,128,128]{1,2,0:T(8,128)} custom-call(f32[4,128,128]{2,1,0:T(8,128)S(1)} %get-tuple-element.32), custom_call_target="InvertDiagBlocksLowerTriangular" | custom-call | tf_op jit(solution)/shard_map/jit(_solve_triangular)/triangular_solve | solution.py:42
  263.3 3.6 all-gather.13.cloned.1.call-done
  266.8 2.9 reduce_sum.69
  280.9 49.1 %all-gather.15.cloned.1.call-done = bf16[8192,256]{1,0:T(8,128)(2,1)} async-done(((bf16[512,256]{1,0:T(8,128)(2,1)}), bf16[8192,256]{1,0:T(8,128)(2,1)}) %all-gather.15.cloned.1.call-update) | async-done | bytes 4194320 | tf_op jit(solution)/shard_map/all_gather | solution.py:13
  330.0 2.9 reduce_sum.70
  337.4 3.8 %all-to-all-start = ((f32[1024,16,16]{0,2,1:T(8,128)}), f32[1024,16,16]{0,2,1:T(8,128)S(1)}, u32[]{:S(2)}, u32[]{:S(2)}) async-start(f32[1024,16,16]{0,2,1:T(8,128)} %all_to_all.12), calls=%async_computation | async-start | bytes 2097152 | tf_op jit(solution)/shard_map/all_to_all | solution.py:58
  341.4 24.8 %all-to-all-done = f32[1024,16,16]{0,2,1:T(8,128)S(1)} async-done(((f32[1024,16,16]{0,2,1:T(8,128)}), f32[1024,16,16]{0,2,1:T(8,128)S(1)}, u32[]{:S(2)}, u32[]{:S(2)}) %all-to-all-start) | async-done | bytes 1048608 | tf_op jit(solution)/shard_map/all_to_all | solution.py:58
  (129 shorter events, 79.4 us)
Async XLA Ops:
  7.2 122.6 %all-gather.9.cloned.1.call-start = ((), (), s32[]{:S(2)}) async-start(), calls=%async_computation.1 | async-start | bytes 4456448 | tf_op jit(solution)/shard_map/all_gather | solution.py:13
  71.5 58.0 %copy-start = (s32[32]{0:T(128)S(1)}, s32[32]{0:T(128)}, u32[]{:S(2)}) copy-start(s32[32]{0:T(128)} %param.9) | copy-start | bytes 388
  75.7 123.6 %all-gather.11.cloned.1.call-start = ((), (), s32[]{:S(2)}) async-start(), calls=%async_computation.2 | async-start | bytes 4456448 | tf_op jit(solution)/shard_map/all_gather | solution.py:13
  146.5 120.3 %all-gather.13.cloned.1.call-start = ((), (), s32[]{:S(2)}) async-start(), calls=%async_computation.3 | async-start | bytes 4456448 | tf_op jit(solution)/shard_map/all_gather | solution.py:13
  214.2 115.8 %all-gather.15.cloned.1.call-start = ((), (), s32[]{:S(2)}) async-start(), calls=%async_computation.4 | async-start | bytes 4456448 | tf_op jit(solution)/shard_map/all_gather | solution.py:13
  337.4 28.8 %all-to-all-start = ((f32[1024,16,16]{0,2,1:T(8,128)}), f32[1024,16,16]{0,2,1:T(8,128)S(1)}, u32[]{:S(2)}, u32[]{:S(2)}) async-start(f32[1024,16,16]{0,2,1:T(8,128)} %all_to_all.12), calls=%async_computation | async-start | bytes 2097152 | tf_op jit(solution)/shard_map/all_to_all | solution.py:58
Sparse Core Ops, SparseCore 0:
  75.8 52.3 all-gather.8
  146.6 52.2 all-gather.10
  214.3 52.4 all-gather.12
  281.0 48.9 all-gather.14
